TPU v7x, 256 devices: a whole 4x4x8 slice. The times are simulated.
256 devices in a mesh: tower: 16 (over z_lo, y, core), dev: 16 (over z_hi, x).
Axes of the slice: x: 4, y: 4, z: 8 (z_hi: 4, z_lo: 2; z = z_hi * 2 + z_lo), core: 2. Of those that a mesh axis runs over, the one named last changes fastest.
Arguments:
- bag_ids: int32 [16, 8192, 32, 4], P('tower', None, 'dev'), may hold values from 0 to 1023
- bag_lengths: int32 [16, 8192, 32], P('tower', None, 'dev'), may hold values from 1 to 4
- tables: bfloat16 [16, 32, 1024, 128], P('tower', 'dev'), may hold values from -3 to 3
- cross_down: bfloat16 [16, 1, 4096, 512], P('tower'), may hold values from -0.09375 to 0.09375
- cross_up: bfloat16 [16, 1, 512, 4096], P('tower'), may hold values from -0.25 to 0.25
- cross_bias: float32 [16, 1, 4096], P('tower'), may hold values from -4 to 4
- proj_weight: bfloat16 [16, 4096, 512], P('tower'), may hold values from -0.09375 to 0.09375
- proj_bias: float32 [16, 512], P('tower'), may hold values from -3 to 3
Outputs:
- interactions: float32 [8192, 120], P(('tower', 'dev'))
Inputs may be any that keep to these rules, and one draw needn't show every extreme that they name: `bag_ids`: where table rows travel between devices, each is sent as a whole 32-bit integer, one to a slot; a program may not pack several table rows into one word. `bag_lengths`: where bag lengths travel between devices, a program may pack several of them into one word.
All inputs are finite; a program needn't handle non-finite values.
Results may differ from a plain program's by a relative error of at most 0.0071.
Values may be sent and summed in bfloat16 or wider, within the bound.
A program may use at most 128 MiB of HBM per device.

v0:
```python
import jax
import jax.numpy as jnp
import numpy as np
from jax import lax
from jax.sharding import PartitionSpec as P

EMB = 128
OUT = 512


def pool_rows(tables_one, ids_one, lengths_one):
    table_rows = tables_one.shape[1]
    positions = lax.iota(jnp.int32, table_rows)
    counts = jnp.zeros(ids_one.shape[:2] + (table_rows,), jnp.bfloat16)
    for slot_index in range(ids_one.shape[2]):
        matched = (ids_one[:, :, slot_index, None] == positions) & (slot_index < lengths_one)[
            :, :, None
        ]
        counts = counts + matched.astype(jnp.bfloat16)
    summed = jnp.einsum("sft,ftd->sfd", counts, tables_one, preferred_element_type=jnp.float32)
    return summed.astype(jnp.bfloat16)


def tower_forward(base, down, up, bias, proj, proj_b):
    base_f = base.astype(jnp.float32)
    cross = base
    low = jnp.dot(cross, down[0], preferred_element_type=jnp.float32).astype(jnp.bfloat16)
    high = jnp.dot(low, up[0], preferred_element_type=jnp.float32) + bias[0]
    cross = (base_f * high + cross.astype(jnp.float32)).astype(jnp.bfloat16)
    return (jnp.dot(cross, proj, preferred_element_type=jnp.float32) + proj_b).astype(jnp.bfloat16)


def local(bag_ids, bag_lengths, tables, cross_down, cross_up, cross_bias, proj_weight, proj_bias):
    towers = lax.axis_size("tower")
    members = lax.axis_size("dev")
    samples = bag_ids.shape[1]
    block = samples // (towers * members)
    feat_dev = bag_ids.shape[2]
    slots = bag_ids.shape[3]
    weights = (cross_down[0], cross_up[0], cross_bias[0], proj_weight[0], proj_bias[0])
    every_table = lax.all_gather(tables[0], "dev", axis=0, tiled=True)
    keyed = bag_ids[0].reshape(towers, members, block, feat_dev, slots)
    counted = bag_lengths[0].reshape(towers, members, block, feat_dev)
    index = lax.all_to_all(keyed, "dev", split_axis=1, concat_axis=3, tiled=True)
    lengths_here = lax.all_to_all(counted, "dev", split_axis=1, concat_axis=3, tiled=True)
    count = index.shape[2]
    pooled = pool_rows(
        every_table,
        index.reshape(towers * count, -1, slots),
        lengths_here.reshape(towers * count, -1),
    )
    pooled_block = pooled.reshape(towers, 1, count, -1, EMB)
    finish_count = pooled_block.shape[2]
    rows = pooled_block.reshape(towers * finish_count, -1)
    outputs = tower_forward(rows, *weights).reshape(towers, finish_count, -1)
    gathered = lax.all_to_all(outputs, "tower", split_axis=0, concat_axis=0, tiled=True)
    gram = jnp.einsum(
        "isk,jsk->sij", gathered, gathered, preferred_element_type=jnp.float32
    ) / jnp.sqrt(jnp.float32(OUT))
    upper, lower = np.triu_indices(towers, 1)
    return gram[:, upper, lower]


def solution(mesh):
    placed = (
        P("tower", None, "dev", None),
        P("tower", None, "dev"),
        P("tower", "dev", None, None),
        P("tower", None, None, None),
        P("tower", None, None, None),
        P("tower", None, None),
        P("tower", None, None),
        P("tower", None),
    )
    return jax.shard_map(
        local, mesh=mesh, in_specs=placed, out_specs=P(("tower", "dev"), None), check_vma=False
    )
```

profile of v0, /device:TPU:1, one launch (start us, length us, event | category | flops | bytes accessed | tf_op | source)
XLA Modules:
  0.0 205.6 jit_solution(1138326824918847656)
XLA Ops:
  6.5 0.7 all-gather.3.cloned.1.call-update
  7.3 1.0 reshape_squeeze.7
  8.4 0.8 reshape.57
  9.1 11.6 %all-to-all-start.1 = ((s32[16,1,1024]{2,1,0:T(1,128)}), s32[16,1,1024]{2,1,0:T(1,128)S(1)}, u32[]{:S(2)}, u32[]{:S(2)}) async-start(s32[16,1,1024]{2,1,0:T(1,128)} %reshape.57), calls=%async_computation.1 | async-start | bytes 131072 | tf_op jit(solution)/shard_map/all_to_all | solution.py:45
  20.7 1.3 reshape_squeeze.6
  22.0 0.3 copy.46
  22.4 1.2 reshape.55
  23.5 6.1 %all-to-all-done.1 = s32[16,1,1024]{2,1,0:T(1,128)S(1)} async-done(((s32[16,1,1024]{2,1,0:T(1,128)}), s32[16,1,1024]{2,1,0:T(1,128)S(1)}, u32[]{:S(2)}, u32[]{:S(2)}) %all-to-all-start.1) | async-done | bytes 65568 | tf_op jit(solution)/shard_map/all_to_all | solution.py:45
  29.7 3.5 %all-to-all-start = ((s32[16,1,4096]{2,1,0:T(1,128)}), s32[16,1,4096]{2,1,0:T(1,128)S(1)}, u32[]{:S(2)}, u32[]{:S(2)}) async-start(s32[16,1,4096]{2,1,0:T(1,128)} %reshape.55), calls=%async_computation | async-start | bytes 524288 | tf_op jit(solution)/shard_map/all_to_all | solution.py:44
  33.2 0.5 broadcast.60
  33.7 0.8 reduce.1
  34.5 0.1 reshape.58
  34.6 0.1 compare_bitcast_fusion.3
  34.8 0.2 gt.80
  34.9 0.2 gt.95
  35.1 0.2 gt.90
  35.2 0.2 gt.85
  35.4 17.6 %all-to-all-done = s32[16,1,4096]{2,1,0:T(1,128)S(1)} async-done(((s32[16,1,4096]{2,1,0:T(1,128)}), s32[16,1,4096]{2,1,0:T(1,128)S(1)}, u32[]{:S(2)}, u32[]{:S(2)}) %all-to-all-start) | async-done | bytes 262176 | tf_op jit(solution)/shard_map/all_to_all | solution.py:44
  53.0 1.3 reduce
  54.2 0.3 reshape.56
  54.8 0.4 reshape.46
  55.2 57.7 %fusion.53 = bf16[512,32,1024]{2,0,1:T(8,128)(2,1)} fusion(s32[512,32]{0,1:T(8,128)S(1)} %get-tuple-element.10, s32[512,32]{0,1:T(8,128)S(1)} %get-tuple-element.11, s32[512,32]{0,1:T(8,128)S(1)} %get-tuple-element.12, s32[512,32]{0,1:T(8,128)S(1)} %get-tuple-element.9, pred[512,32]{0,1:T(8,128)(4,1)S(1)} %gt.95, ...), kind=kLoop, calls=%fused_computation.13.clone.clone.clone.clone.1 | loop fusion | flops 335544320 | bytes 33882112 | tf_op jit(solution)/shard_map/sft,ftd->sfd/dot_general | solution.py:20
  113.0 14.5 %all-gather.3.cloned.1.call-done = bf16[1,32,1024,128]{3,2,0,1:T(8,128)(2,1)} async-done(((bf16[1,2,1024,128]{3,2,0,1:T(8,128)(2,1)}), bf16[1,32,1024,128]{3,2,0,1:T(8,128)(2,1)}) %all-gather.3.cloned.1.call-update) | async-done | bytes 8388624 | tf_op jit(solution)/shard_map/all_gather | solution.py:41
  127.5 18.9 %fusion.31 = bf16[32,512,128]{1,2,0:T(8,128)(2,1)} fusion(bf16[1,32,1024,128]{3,2,0,1:T(8,128)(2,1)} %all-gather.3.cloned.1.call-done, bf16[512,32,1024]{2,0,1:T(8,128)(2,1)} %fusion.53), kind=kOutput, calls=%fused_computation.33 | convolution fusion | flops 4297064448 | bytes 46137344 | tf_op jit(solution)/shard_map/sft,ftd->sfd/dot_general | solution.py:20
  146.3 6.4 %copy.37 = bf16[512,4096]{1,0:T(8,128)(2,1)} copy(bf16[512,4096]{0,1:T(8,128)(2,1)} %bitcast.98) | data formatting | bytes 8388608 | tf_op jit(solution)/shard_map/reshape;reshape | solution.py:54
  152.8 12.7 %fusion.24 = bf16[512,4096]{1,0:T(8,128)(2,1)} fusion(bf16[512,4096]{1,0:T(8,128)(2,1)} %copy.37, bf16[1,1,512,4096]{3,2,1,0:T(8,128)(2,1)} %param.16, f32[4096]{0:T(1024)S(1)} %bitcast.104, bf16[512,4096]{0,1:T(8,128)(2,1)} %bitcast.99, bf16[1,1,4096,512]{3,2,1,0:T(8,128)(2,1)} %param.15), kind=kOutput, calls=%fused_computation.26 | convolution fusion | flops 4305715200 | bytes 20987904 | tf_op jit(solution)/shard_map/dot_general | solution.py:28
  165.5 5.8 %fusion.39 = bf16[512,512]{1,0:T(8,128)(2,1)S(1)} fusion(bf16[512,4096]{1,0:T(8,128)(2,1)} %fusion.24, bf16[1,4096,512]{2,1,0:T(8,128)(2,1)} %param.18, f32[512]{0:T(512)S(1)} %bitcast.105), kind=kOutput, calls=%fused_computation.35 | convolution fusion | flops 2148007936 | bytes 8914944 | tf_op jit(solution)/shard_map/dot_general | solution.py:30
  171.3 24.6 %all_to_all.29 = bf16[16,32,512]{2,1,0:T(8,128)(2,1)S(1)} all-to-all(bf16[16,32,512]{2,1,0:T(8,128)(2,1)S(1)} %bitcast.102), channel_id=1, replica_groups=mesh['tower'=16,'dev'=16] {'tower'}, dimensions={0} | all-to-all | bytes 1048576 | tf_op jit(solution)/shard_map/all_to_all | solution.py:56
  195.9 0.4 convolution_multiply_fusion
  196.3 0.2 copy.40
  196.5 1.6 gather_fusion
  198.1 0.7 copy.41
  (11 shorter events, 0.3 us)
Async XLA Ops:
  6.5 120.9 %all-gather.3.cloned.1.call-start = ((), (), s32[]{:S(2)}) async-start(), calls=%async_computation.3 | async-start | bytes 8912896 | tf_op jit(solution)/shard_map/all_gather | solution.py:41
  9.1 20.5 %all-to-all-start.1 = ((s32[16,1,1024]{2,1,0:T(1,128)}), s32[16,1,1024]{2,1,0:T(1,128)S(1)}, u32[]{:S(2)}, u32[]{:S(2)}) async-start(s32[16,1,1024]{2,1,0:T(1,128)} %reshape.57), calls=%async_computation.1 | async-start | bytes 131072 | tf_op jit(solution)/shard_map/all_to_all | solution.py:45
  29.7 23.3 %all-to-all-start = ((s32[16,1,4096]{2,1,0:T(1,128)}), s32[16,1,4096]{2,1,0:T(1,128)S(1)}, u32[]{:S(2)}, u32[]{:S(2)}) async-start(s32[16,1,4096]{2,1,0:T(1,128)} %reshape.55), calls=%async_computation | async-start | bytes 524288 | tf_op jit(solution)/shard_map/all_to_all | solution.py:44
  146.3 6.5 %copy-start.1 = (f32[1,1,4096]{2,1,0:T(1,128)S(1)}, f32[1,1,4096]{2,1,0:T(1,128)}, u32[]{:S(2)}) copy-start(f32[1,1,4096]{2,1,0:T(1,128)} %param.17) | copy-start | bytes 49156
  152.8 12.7 %copy-start.2 = (f32[1,512]{1,0:T(1,128)S(1)}, f32[1,512]{1,0:T(1,128)}, u32[]{:S(2)}) copy-start(f32[1,512]{1,0:T(1,128)} %param.19) | copy-start | bytes 6148
  165.5 31.0 %copy-start = (s32[120]{0:T(128)S(1)}, s32[120]{0:T(128)}, u32[]{:S(2)}) copy-start(s32[120]{0:T(128)} %constant.53) | copy-start | bytes 1444
Sparse Core Ops, SparseCore 0:
  9.8 117.6 all-gather.2
where the time goes:
time: 206 us
  other arithmetic  59.9 us (29%)
  waiting for transfers between devices  38.9 us (19%)
  matrix products  37.8 us (18%)
  blocking collectives  24.6 us (12%)
  local copies, waits for them, and re-layouts  15.8 us (8%)
  starting transfers between devices  15.1 us (7%)
  between operations  13.5 us (7%)
    dot_general x1, other arithmetic, pool_rows(): jnp.einsum('sft,ftd->sfd', counts, tables_one, preferred_element_type=jnp...  57.7 us
    all_to_all x1, blocking collectives, local(): lax.all_to_all(outputs, 'tower', split_axis=0, concat_axis=0, tiled=True)  24.6 us
    dot_general x1, matrix products, pool_rows(): jnp.einsum('sft,ftd->sfd', counts, tables_one, preferred_element_type=jnp...  18.9 us
    all_to_all x1, waiting for transfers between devices, local(): lax.all_to_all(keyed, 'dev', split_axis=1, concat_axis=3, tiled=True)  17.6 us
    all_gather x1, waiting for transfers between devices, local(): every_table = lax.all_gather(tables[0], 'dev', axis=0, tiled=True)  14.5 us
    dot_general x1, matrix products, tower_forward(): high = jnp.dot(low, up[0], preferred_element_type=jnp.float32) + bias[0]  12.7 us
    all_to_all x1, starting transfers between devices, local(): lax.all_to_all(counted, 'dev', split_axis=1, concat_axis=3, tiled=True)  11.6 us
    another operation x1, local copies, waits for them, and re-layouts, local(): rows = pooled_block.reshape(towers * finish_count, -1)  6.45 us
  transfers between devices with their start and end apart: 3, of which 3 were waited for; matrix products, arithmetic and copies ran while one was open for 32% of the time, Pallas kernels for 0%

commit v1 on v0

--- a/solution.py
+++ b/solution.py
@@ -38,7 +38,9 @@
     feat_dev = bag_ids.shape[2]
     slots = bag_ids.shape[3]
     weights = (cross_down[0], cross_up[0], cross_bias[0], proj_weight[0], proj_bias[0])
-    every_table = lax.all_gather(tables[0], "dev", axis=0, tiled=True)
+    every_table = jnp.concatenate(
+        lax.all_to_all(jnp.stack([tables[0]] * lax.axis_size("dev")), "dev", 0, 0), axis=0
+    )
     keyed = bag_ids[0].reshape(towers, members, block, feat_dev, slots)
     counted = bag_lengths[0].reshape(towers, members, block, feat_dev)
     index = lax.all_to_all(keyed, "dev", split_axis=1, concat_axis=3, tiled=True)

time: 206 us -> 302 us (1.47)
  waiting for transfers between devices: 38.9 us -> 141 us
  between operations: 13.5 us -> 0.14 us
  local copies, waits for them, and re-layouts: 15.8 us -> 21.2 us
  starting transfers between devices: 15.1 us -> 20 us
  blocking collectives: 24.6 us -> 20.3 us
    all_to_all x0 -> x1, waiting for transfers between devices: none -> 126 us  [local(): lax.all_to_all(jnp.stack([tables[0]] * lax.axis_size('dev')), 'dev', 0, 0)]
    all_gather x1 -> x0, waiting for transfers between devices: 14.5 us -> none  [local(): every_table = lax.all_gather(tables[0], 'dev', axis=0, tiled=True)]
    all_to_all x1, waiting for transfers between devices: 17.6 us -> 8.91 us  [local(): lax.all_to_all(keyed, 'dev', split_axis=1, concat_axis=3, tiled=True)]
    another operation x0 -> x2, local copies, waits for them, and re-layouts: none -> 5.52 us  [the longest x1 4.28 us: local(): jnp.stack([tables[0]] * lax.axis_size('dev'))]
    all_to_all x0 -> x1, starting transfers between devices: none -> 4.94 us  [local(): lax.all_to_all(jnp.stack([tables[0]] * lax.axis_size('dev')), 'dev', 0, 0)]
    all_to_all x1, blocking collectives: 24.6 us -> 20.3 us  [local(): lax.all_to_all(outputs, 'tower', split_axis=0, concat_axis=0, tiled=True)]
  transfers between devices with their start and end apart: 3 -> 3, of which waited for: 3 -> 3; matrix products, arithmetic and copies ran while one was open for 32% -> 22% of each run, Pallas kernels for 0% -> 0%
where the time goes in v1:
time: 302 us
  waiting for transfers between devices  141 us (47%)
  other arithmetic  59.9 us (20%)
  matrix products  38.6 us (13%)
  local copies, waits for them, and re-layouts  21.2 us (7%)
  blocking collectives  20.3 us (7%)
  starting transfers between devices  20 us (7%)
    all_to_all x1, waiting for transfers between devices, local(): lax.all_to_all(jnp.stack([tables[0]] * lax.axis_size('dev')), 'dev', 0, 0)  126 us
    dot_general x1, other arithmetic, pool_rows(): jnp.einsum('sft,ftd->sfd', counts, tables_one, preferred_element_type=jnp...  57.7 us
    all_to_all x1, blocking collectives, local(): lax.all_to_all(outputs, 'tower', split_axis=0, concat_axis=0, tiled=True)  20.3 us
    dot_general x1, matrix products, pool_rows(): jnp.einsum('sft,ftd->sfd', counts, tables_one, preferred_element_type=jnp...  19.7 us
    dot_general x1, matrix products, tower_forward(): high = jnp.dot(low, up[0], preferred_element_type=jnp.float32) + bias[0]  12.7 us
    all_to_all x1, starting transfers between devices, local(): lax.all_to_all(counted, 'dev', split_axis=1, concat_axis=3, tiled=True)  11.6 us
    all_to_all x1, waiting for transfers between devices, local(): lax.all_to_all(keyed, 'dev', split_axis=1, concat_axis=3, tiled=True)  8.91 us
    another operation x1, local copies, waits for them, and re-layouts, local(): rows = pooled_block.reshape(towers * finish_count, -1)  6.4 us
  transfers between devices with their start and end apart: 3, of which 3 were waited for; matrix products, arithmetic and copies ran while one was open for 22% of the time, Pallas kernels for 0%

profile of v1, /device:TPU:1, one launch (start us, length us, event | category | flops | bytes accessed | tf_op | source)
XLA Modules:
  0.0 301.6 jit_solution(15151791337683636980)
XLA Ops:
  0.0 1.0 reshape_squeeze.7
  1.1 0.8 reshape.61
  1.9 11.6 %all-to-all-start.1 = ((s32[16,1,1024]{2,1,0:T(1,128)}), s32[16,1,1024]{2,1,0:T(1,128)S(1)}, u32[]{:S(2)}, u32[]{:S(2)}) async-start(s32[16,1,1024]{2,1,0:T(1,128)} %reshape.61), calls=%async_computation.1 | async-start | bytes 131072 | tf_op jit(solution)/shard_map/all_to_all | solution.py:47
  13.5 1.3 reshape_squeeze.6
  14.8 0.3 copy.44
  15.1 1.2 reshape.59
  16.3 6.1 %all-to-all-done.1 = s32[16,1,1024]{2,1,0:T(1,128)S(1)} async-done(((s32[16,1,1024]{2,1,0:T(1,128)}), s32[16,1,1024]{2,1,0:T(1,128)S(1)}, u32[]{:S(2)}, u32[]{:S(2)}) %all-to-all-start.1) | async-done | bytes 65568 | tf_op jit(solution)/shard_map/all_to_all | solution.py:47
  22.4 3.5 %all-to-all-start = ((s32[16,1,4096]{2,1,0:T(1,128)}), s32[16,1,4096]{2,1,0:T(1,128)S(1)}, u32[]{:S(2)}, u32[]{:S(2)}) async-start(s32[16,1,4096]{2,1,0:T(1,128)} %reshape.59), calls=%async_computation | async-start | bytes 524288 | tf_op jit(solution)/shard_map/all_to_all | solution.py:46
  25.9 1.2 copy.34
  27.2 8.9 %all-to-all-done = s32[16,1,4096]{2,1,0:T(1,128)S(1)} async-done(((s32[16,1,4096]{2,1,0:T(1,128)}), s32[16,1,4096]{2,1,0:T(1,128)S(1)}, u32[]{:S(2)}, u32[]{:S(2)}) %all-to-all-start) | async-done | bytes 262176 | tf_op jit(solution)/shard_map/all_to_all | solution.py:46
  36.1 4.3 %stack.3 = bf16[16,2,1024,128]{2,3,1,0:T(8,128)(2,1)} broadcast(bf16[2,1024,128]{1,2,0:T(8,128)(2,1)S(1)} %copy.34), dimensions={1,2,3} | broadcast | bytes 8912896 | tf_op jit(solution)/shard_map/stack | solution.py:42
  40.4 4.9 %all-to-all-start.2 = ((bf16[16,2,1024,128]{2,3,1,0:T(8,128)(2,1)}), bf16[16,2,1024,128]{2,3,1,0:T(8,128)(2,1)}, u32[]{:S(2)}, u32[]{:S(2)}) async-start(bf16[16,2,1024,128]{2,3,1,0:T(8,128)(2,1)} %stack.3), calls=%async_computation.2 | async-start | bytes 16777216 | tf_op jit(solution)/shard_map/all_to_all | solution.py:42
  45.3 0.5 broadcast.61
  45.8 0.8 reduce.1
  46.9 0.2 gt.80
  47.1 0.2 gt.95
  47.2 0.2 gt.90
  47.4 0.2 gt.85
  47.5 1.3 reduce
  48.8 0.3 reshape.60
  49.3 0.4 reshape.50
  49.8 57.7 %fusion.51 = bf16[512,32,1024]{2,0,1:T(8,128)(2,1)} fusion(s32[512,32]{0,1:T(8,128)S(1)} %get-tuple-element.10, s32[512,32]{0,1:T(8,128)S(1)} %get-tuple-element.11, s32[512,32]{0,1:T(8,128)S(1)} %get-tuple-element.12, s32[512,32]{0,1:T(8,128)S(1)} %get-tuple-element.9, pred[512,32]{0,1:T(8,128)(4,1)S(1)} %gt.95, ...), kind=kLoop, calls=%fused_computation.13.clone.clone.clone.clone.1 | loop fusion | flops 335544320 | bytes 33882112 | tf_op jit(solution)/shard_map/sft,ftd->sfd/dot_general | solution.py:20
  107.5 126.4 %all-to-all-done.2 = bf16[16,2,1024,128]{2,3,1,0:T(8,128)(2,1)} async-done(((bf16[16,2,1024,128]{2,3,1,0:T(8,128)(2,1)}), bf16[16,2,1024,128]{2,3,1,0:T(8,128)(2,1)}, u32[]{:S(2)}, u32[]{:S(2)}) %all-to-all-start.2) | async-done | bytes 8388640 | tf_op jit(solution)/shard_map/all_to_all | solution.py:42
  233.9 19.7 %fusion.30 = bf16[32,512,128]{1,2,0:T(8,128)(2,1)} fusion(bf16[32,1024,128]{1,2,0:T(8,128)(2,1)} %bitcast.15, bf16[512,32,1024]{2,0,1:T(8,128)(2,1)} %fusion.51), kind=kOutput, calls=%fused_computation.32 | convolution fusion | flops 4297064448 | bytes 46137344 | tf_op jit(solution)/shard_map/sft,ftd->sfd/dot_general | solution.py:20
  253.6 6.4 %copy.35 = bf16[512,4096]{1,0:T(8,128)(2,1)} copy(bf16[512,4096]{0,1:T(8,128)(2,1)} %bitcast.94) | data formatting | bytes 8388608 | tf_op jit(solution)/shard_map/reshape;reshape | solution.py:56
  260.0 12.7 %fusion.24 = bf16[512,4096]{1,0:T(8,128)(2,1)} fusion(bf16[512,4096]{1,0:T(8,128)(2,1)} %copy.35, bf16[1,1,512,4096]{3,2,1,0:T(8,128)(2,1)} %param.16, f32[4096]{0:T(1024)S(1)} %bitcast.100, bf16[512,4096]{0,1:T(8,128)(2,1)} %bitcast.95, bf16[1,1,4096,512]{3,2,1,0:T(8,128)(2,1)} %param.15), kind=kOutput, calls=%fused_computation.26 | convolution fusion | flops 4305715200 | bytes 20987904 | tf_op jit(solution)/shard_map/dot_general | solution.py:28
  272.7 5.8 %fusion.36 = bf16[512,512]{1,0:T(8,128)(2,1)S(1)} fusion(bf16[512,4096]{1,0:T(8,128)(2,1)} %fusion.24, bf16[1,4096,512]{2,1,0:T(8,128)(2,1)} %param.18, f32[512]{0:T(512)S(1)} %bitcast.101), kind=kOutput, calls=%fused_computation.34 | convolution fusion | flops 2148007936 | bytes 8914944 | tf_op jit(solution)/shard_map/dot_general | solution.py:30
  278.5 20.3 %all_to_all.34 = bf16[16,32,512]{2,1,0:T(8,128)(2,1)S(1)} all-to-all(bf16[16,32,512]{2,1,0:T(8,128)(2,1)S(1)} %bitcast.98), channel_id=1, replica_groups=mesh['tower'=16,'dev'=16] {'tower'}, dimensions={0} | all-to-all | bytes 1048576 | tf_op jit(solution)/shard_map/all_to_all | solution.py:58
  298.8 0.4 convolution_multiply_fusion
  299.2 0.2 copy.38
  299.4 1.6 gather_fusion
  301.0 0.7 copy.39
  (12 shorter events, 0.5 us)
Async XLA Ops:
  1.9 20.5 %all-to-all-start.1 = ((s32[16,1,1024]{2,1,0:T(1,128)}), s32[16,1,1024]{2,1,0:T(1,128)S(1)}, u32[]{:S(2)}, u32[]{:S(2)}) async-start(s32[16,1,1024]{2,1,0:T(1,128)} %reshape.61), calls=%async_computation.1 | async-start | bytes 131072 | tf_op jit(solution)/shard_map/all_to_all | solution.py:47
  22.4 13.7 %all-to-all-start = ((s32[16,1,4096]{2,1,0:T(1,128)}), s32[16,1,4096]{2,1,0:T(1,128)S(1)}, u32[]{:S(2)}, u32[]{:S(2)}) async-start(s32[16,1,4096]{2,1,0:T(1,128)} %reshape.59), calls=%async_computation | async-start | bytes 524288 | tf_op jit(solution)/shard_map/all_to_all | solution.py:46
  40.4 193.5 %all-to-all-start.2 = ((bf16[16,2,1024,128]{2,3,1,0:T(8,128)(2,1)}), bf16[16,2,1024,128]{2,3,1,0:T(8,128)(2,1)}, u32[]{:S(2)}, u32[]{:S(2)}) async-start(bf16[16,2,1024,128]{2,3,1,0:T(8,128)(2,1)} %stack.3), calls=%async_computation.2 | async-start | bytes 16777216 | tf_op jit(solution)/shard_map/all_to_all | solution.py:42
  253.6 6.4 %copy-start.1 = (f32[1,1,4096]{2,1,0:T(1,128)S(1)}, f32[1,1,4096]{2,1,0:T(1,128)}, u32[]{:S(2)}) copy-start(f32[1,1,4096]{2,1,0:T(1,128)} %param.17) | copy-start | bytes 49156
  260.0 12.7 %copy-start.2 = (f32[1,512]{1,0:T(1,128)S(1)}, f32[1,512]{1,0:T(1,128)}, u32[]{:S(2)}) copy-start(f32[1,512]{1,0:T(1,128)} %param.19) | copy-start | bytes 6148
  272.7 26.6 %copy-start = (s32[120]{0:T(128)S(1)}, s32[120]{0:T(128)}, u32[]{:S(2)}) copy-start(s32[120]{0:T(128)} %constant.53) | copy-start | bytes 1444
